TPU v7x, 512 devices: a whole 4x8x8 slice. The times are simulated.
512 devices in a mesh: sample: 4 (over y_lo), variant: 32 (over x, z), trait: 4 (over y_hi, core).
Axes of the slice: x: 4, y: 8 (y_hi: 2, y_lo: 4; y = y_hi * 4 + y_lo), z: 8, core: 2. Of those that a mesh axis runs over, the one named last changes fastest.
Arguments:
- dosages: bfloat16 [4096, 65536], P('sample', 'variant')
- phenotypes: float32 [4096, 64], P('sample', 'trait')
- batch_rows: int32 [8, 4096], P(None, 'sample'), may hold values from 0 to 1023
Outputs:
- weights: float32 [64, 65536], P('trait', 'variant')
Inputs may be any that keep to these rules, and one draw needn't show every extreme that they name: Draw j of iteration t refers to sample (j // 1024) * 1024 + batch_rows[t-1, j]; draws repeat.
All inputs are finite; a program needn't handle non-finite values.
Results may differ from a plain program's by a relative error of at most 0.0025.
Values may be sent and summed in bfloat16 or wider, within the bound.
A program may use at most 64 MiB of HBM per device.

v0:
```python
import math
import jax
import jax.numpy as jnp
from jax import lax
from jax.sharding import PartitionSpec as P

ITERS = 8


def trait_power(dual):
    squares = jnp.sum(dual * dual, axis=0)
    return lax.psum(squares, "trait")


def on_device(dosages, phenotypes, batch_rows):
    local_rows = dosages.shape[0]
    group_size = lax.axis_size("sample")
    total_variants = dosages.shape[1] * lax.axis_size("variant")
    total_draws = batch_rows.shape[1] * group_size
    pred_scale = 0.06 * math.sqrt(total_draws) / total_variants
    grad_scale = 1.0 / math.sqrt(total_draws)
    width_traits = phenotypes.shape[1]
    width_cols = dosages.shape[1]
    dual = jnp.zeros((width_traits, width_cols), jnp.float32)
    weights_full = jnp.zeros((width_traits, width_cols), jnp.float32)
    weights_low = weights_full.astype(jnp.bfloat16)
    for step in range(ITERS):
        turn = step + 1
        counts = jnp.zeros((local_rows,), jnp.float32).at[batch_rows[step]].add(1.0)
        if step == 0:
            predictions = jnp.zeros_like(phenotypes)
        else:
            partial_sum = lax.dot_general(
                dosages, weights_low, (((1,), (1,)), ((), ())), preferred_element_type=jnp.float32
            )
            predictions = (
                lax.psum(partial_sum.astype(jnp.bfloat16), "variant").astype(jnp.float32)
                * pred_scale
            )
        misfit = (counts[:, None] * (predictions - phenotypes)).astype(jnp.bfloat16)
        grad_part = lax.dot_general(
            misfit, dosages, (((0,), (0,)), ((), ())), preferred_element_type=jnp.float32
        )
        gradient = lax.psum(grad_part, "sample") * grad_scale
        dual = dual + (gradient - dual) / turn
        power = trait_power(dual)
        shrink = jax.nn.relu(1.0 - 20.0 / jnp.sqrt(power + 1e-05))
        weights_full = -math.sqrt(turn) * shrink[None, :] * dual
        weights_low = weights_full.astype(jnp.bfloat16)
    return weights_full


def solution(mesh):
    return jax.shard_map(
        on_device,
        mesh=mesh,
        in_specs=(P("sample", "variant"), P("sample", "trait"), P(None, "sample")),
        out_specs=P("trait", "variant"),
        check_vma=False,
    )
```

profile of v0, /device:TPU:1, one launch (start us, length us, event | category | flops | bytes accessed | tf_op | source)
XLA Modules:
  0.0 1546.0 jit_solution(12416131265628424412)
XLA Ops:
  7.6 7.6 scatter_custom_fusion
  15.3 3.6 fusion.14
  18.9 7.6 scatter_custom_fusion.1
  26.6 49.9 %all-reduce.9.cloned.1.call-done = f32[16,2048]{1,0:T(8,128)} async-done(((f32[16,2048]{1,0:T(8,128)}), f32[16,2048]{1,0:T(8,128)}) %all-reduce.9.cloned.1.call-update) | async-done | bytes 131088 | tf_op jit(solution)/shard_map/psum | solution.py:44
  77.4 11.7 psum.162
  92.7 116.2 %psum.163 = bf16[1024,16]{0,1:T(8,128)(2,1)S(1)} all-reduce(bf16[1024,16]{0,1:T(8,128)(2,1)S(1)} %fusion), channel_id=1, replica_groups=mesh['sample'=4,'variant'=32,'trait'=4] {'variant'}, use_global_device_ids=true, to_apply=%region_5.6 | all-reduce | flops 16384 | bytes 65536 | tf_op jit(solution)/shard_map/psum | solution.py:37
  212.4 7.6 scatter_custom_fusion.2
  220.1 63.4 %all-reduce.11.cloned.1.call-done = f32[16,2048]{1,0:T(8,128)} async-done(((f32[16,2048]{1,0:T(8,128)}), f32[16,2048]{1,0:T(8,128)}) %all-reduce.11.cloned.1.call-update) | async-done | bytes 131088 | tf_op jit(solution)/shard_map/psum | solution.py:44
  284.4 11.7 psum.165
  299.5 116.2 %psum.166 = bf16[1024,16]{0,1:T(8,128)(2,1)S(1)} all-reduce(bf16[1024,16]{0,1:T(8,128)(2,1)S(1)} %fusion.1), channel_id=1, replica_groups=mesh['sample'=4,'variant'=32,'trait'=4] {'variant'}, use_global_device_ids=true, to_apply=%region_10.11 | all-reduce | flops 16384 | bytes 65536 | tf_op jit(solution)/shard_map/psum | solution.py:37
  419.3 7.6 scatter_custom_fusion.3
  426.9 63.4 %all-reduce.13.cloned.1.call-done = f32[16,2048]{1,0:T(8,128)} async-done(((f32[16,2048]{1,0:T(8,128)}), f32[16,2048]{1,0:T(8,128)}) %all-reduce.13.cloned.1.call-update) | async-done | bytes 131088 | tf_op jit(solution)/shard_map/psum | solution.py:44
  491.3 11.7 psum.168
  506.5 116.2 %psum.169 = bf16[1024,16]{0,1:T(8,128)(2,1)S(1)} all-reduce(bf16[1024,16]{0,1:T(8,128)(2,1)S(1)} %fusion.2), channel_id=1, replica_groups=mesh['sample'=4,'variant'=32,'trait'=4] {'variant'}, use_global_device_ids=true, to_apply=%region_15.16 | all-reduce | flops 16384 | bytes 65536 | tf_op jit(solution)/shard_map/psum | solution.py:37
  626.4 7.6 scatter_custom_fusion.4
  634.1 63.2 %all-reduce.15.cloned.1.call-done = f32[16,2048]{1,0:T(8,128)} async-done(((f32[16,2048]{1,0:T(8,128)}), f32[16,2048]{1,0:T(8,128)}) %all-reduce.15.cloned.1.call-update) | async-done | bytes 131088 | tf_op jit(solution)/shard_map/psum | solution.py:44
  698.3 11.7 psum.171
  713.4 116.2 %psum.172 = bf16[1024,16]{0,1:T(8,128)(2,1)S(1)} all-reduce(bf16[1024,16]{0,1:T(8,128)(2,1)S(1)} %fusion.3), channel_id=1, replica_groups=mesh['sample'=4,'variant'=32,'trait'=4] {'variant'}, use_global_device_ids=true, to_apply=%region_20.21 | all-reduce | flops 16384 | bytes 65536 | tf_op jit(solution)/shard_map/psum | solution.py:37
  833.1 7.6 scatter_custom_fusion.5
  840.8 63.4 %all-reduce.17.cloned.1.call-done = f32[16,2048]{1,0:T(8,128)} async-done(((f32[16,2048]{1,0:T(8,128)}), f32[16,2048]{1,0:T(8,128)}) %all-reduce.17.cloned.1.call-update) | async-done | bytes 131088 | tf_op jit(solution)/shard_map/psum | solution.py:44
  905.1 11.7 psum.174
  920.4 116.2 %psum.175 = bf16[1024,16]{0,1:T(8,128)(2,1)S(1)} all-reduce(bf16[1024,16]{0,1:T(8,128)(2,1)S(1)} %fusion.4), channel_id=1, replica_groups=mesh['sample'=4,'variant'=32,'trait'=4] {'variant'}, use_global_device_ids=true, to_apply=%region_25.26 | all-reduce | flops 16384 | bytes 65536 | tf_op jit(solution)/shard_map/psum | solution.py:37
  1040.1 7.6 scatter_custom_fusion.6
  1047.7 63.4 %all-reduce.19.cloned.1.call-done = f32[16,2048]{1,0:T(8,128)} async-done(((f32[16,2048]{1,0:T(8,128)}), f32[16,2048]{1,0:T(8,128)}) %all-reduce.19.cloned.1.call-update) | async-done | bytes 131088 | tf_op jit(solution)/shard_map/psum | solution.py:44
  1112.1 11.7 psum.177
  1127.2 116.2 %psum.178 = bf16[1024,16]{0,1:T(8,128)(2,1)S(1)} all-reduce(bf16[1024,16]{0,1:T(8,128)(2,1)S(1)} %fusion.5), channel_id=1, replica_groups=mesh['sample'=4,'variant'=32,'trait'=4] {'variant'}, use_global_device_ids=true, to_apply=%region_30.31 | all-reduce | flops 16384 | bytes 65536 | tf_op jit(solution)/shard_map/psum | solution.py:37
  1247.0 7.6 scatter_custom_fusion.7
  1254.6 63.4 %all-reduce.21.cloned.1.call-done = f32[16,2048]{1,0:T(8,128)} async-done(((f32[16,2048]{1,0:T(8,128)}), f32[16,2048]{1,0:T(8,128)}) %all-reduce.21.cloned.1.call-update) | async-done | bytes 131088 | tf_op jit(solution)/shard_map/psum | solution.py:44
  1319.0 11.7 psum.180
  1334.1 116.2 %psum.181 = bf16[1024,16]{0,1:T(8,128)(2,1)S(1)} all-reduce(bf16[1024,16]{0,1:T(8,128)(2,1)S(1)} %fusion.6), channel_id=1, replica_groups=mesh['sample'=4,'variant'=32,'trait'=4] {'variant'}, use_global_device_ids=true, to_apply=%region_35.36 | all-reduce | flops 16384 | bytes 65536 | tf_op jit(solution)/shard_map/psum | solution.py:37
  1453.8 71.1 %all-reduce.23.cloned.1.call-done = f32[16,2048]{1,0:T(8,128)} async-done(((f32[16,2048]{1,0:T(8,128)}), f32[16,2048]{1,0:T(8,128)}) %all-reduce.23.cloned.1.call-update) | async-done | bytes 131088 | tf_op jit(solution)/shard_map/psum | solution.py:44
  1525.8 11.7 psum.183
  (57 shorter events, 59.4 us)
Async XLA Ops:
  6.5 70.0 %all-reduce.9.cloned.1.call-start = ((), (), s32[]{:S(2)}) async-start(), calls=%async_computation | async-start | bytes 262144 | tf_op jit(solution)/shard_map/psum | solution.py:44
  15.3 193.6 %copy-start = (f32[1024,16]{0,1:T(8,128)S(1)}, f32[1024,16]{0,1:T(8,128)}, u32[]{:S(2)}) copy-start(f32[1024,16]{0,1:T(8,128)} %param.4) | copy-start | bytes 196612
  18.9 264.6 %all-reduce.11.cloned.1.call-start = ((), (), s32[]{:S(2)}) async-start(), calls=%async_computation.1 | async-start | bytes 262144 | tf_op jit(solution)/shard_map/psum | solution.py:44
  89.2 194.3 %copy-start.1 = (f32[16,2048]{1,0:T(8,128)S(1)}, f32[16,2048]{1,0:T(8,128)}, u32[]{:S(2)}) copy-start(f32[16,2048]{1,0:T(8,128)} %all-reduce.9.cloned.1.call-done) | copy-start | bytes 393220
  212.4 277.9 %all-reduce.13.cloned.1.call-start = ((), (), s32[]{:S(2)}) async-start(), calls=%async_computation.2 | async-start | bytes 262144 | tf_op jit(solution)/shard_map/psum | solution.py:44
  419.2 278.0 %all-reduce.15.cloned.1.call-start = ((), (), s32[]{:S(2)}) async-start(), calls=%async_computation.3 | async-start | bytes 262144 | tf_op jit(solution)/shard_map/psum | solution.py:44
  503.0 194.3 %copy-start.2 = (f32[16,2048]{1,0:T(8,128)S(1)}, f32[16,2048]{1,0:T(8,128)}, u32[]{:S(2)}) copy-start(f32[16,2048]{1,0:T(8,128)} %all-reduce.13.cloned.1.call-done) | copy-start | bytes 393220
  626.2 277.9 %all-reduce.17.cloned.1.call-start = ((), (), s32[]{:S(2)}) async-start(), calls=%async_computation.4 | async-start | bytes 262144 | tf_op jit(solution)/shard_map/psum | solution.py:44
  833.1 278.0 %all-reduce.19.cloned.1.call-start = ((), (), s32[]{:S(2)}) async-start(), calls=%async_computation.5 | async-start | bytes 262144 | tf_op jit(solution)/shard_map/psum | solution.py:44
  916.9 194.3 %copy-start.3 = (f32[16,2048]{1,0:T(8,128)S(1)}, f32[16,2048]{1,0:T(8,128)}, u32[]{:S(2)}) copy-start(f32[16,2048]{1,0:T(8,128)} %all-reduce.17.cloned.1.call-done) | copy-start | bytes 393220
  1040.1 277.9 %all-reduce.21.cloned.1.call-start = ((), (), s32[]{:S(2)}) async-start(), calls=%async_computation.6 | async-start | bytes 262144 | tf_op jit(solution)/shard_map/psum | solution.py:44
  1246.9 277.9 %all-reduce.23.cloned.1.call-start = ((), (), s32[]{:S(2)}) async-start(), calls=%async_computation.7 | async-start | bytes 262144 | tf_op jit(solution)/shard_map/psum | solution.py:44
Sparse Core Ops, SparseCore 0:
  19.0 57.4 all-reduce.8
  212.5 70.9 all-reduce.10
  419.4 70.9 all-reduce.12
  626.3 70.9 all-reduce.14
  833.2 70.9 all-reduce.16
  1040.2 70.9 all-reduce.18
  1247.1 70.9 all-reduce.20
  1453.9 70.9 all-reduce.22
where the time goes:
time: 1550 us
  blocking collectives  907 us (59%)
  waiting for transfers between devices  501 us (32%)
  other arithmetic  71.3 us (5%)
  matrix products  52 us (3%)
    psum x7, blocking collectives, on_device(): lax.psum(partial_sum.astype(jnp.bfloat16), 'variant').astype(jnp.float32)  813 us
    psum x8, waiting for transfers between devices, on_device(): gradient = lax.psum(grad_part, 'sample') * grad_scale  501 us
    psum x8, blocking collectives, trait_power(): return lax.psum(squares, 'trait')  93.8 us
    scatter-add x8, other arithmetic, on_device(): counts = jnp.zeros((local_rows,), jnp.float32).at[batch_rows[step]].add(1.0)  60.9 us
  transfers between devices with their start and end apart: 8, of which 8 were waited for; matrix products, arithmetic and copies ran while one was open for 3% of the time, Pallas kernels for 0%

commit v1 on v0

--- a/solution.py
+++ b/solution.py
@@ -34,7 +34,9 @@
                 dosages, weights_low, (((1,), (1,)), ((), ())), preferred_element_type=jnp.float32
             )
             predictions = (
-                lax.psum(partial_sum.astype(jnp.bfloat16), "variant").astype(jnp.float32)
+                jnp.sum(lax.all_gather(partial_sum.astype(jnp.bfloat16), "variant"), axis=0).astype(
+                    jnp.float32
+                )
                 * pred_scale
             )
         misfit = (counts[:, None] * (predictions - phenotypes)).astype(jnp.bfloat16)

time: 1550 us -> 1170 us (0.75)
  blocking collectives: 907 us -> 93.8 us
  waiting for transfers between devices: 501 us -> 921 us
    psum x7 -> x0, blocking collectives: 813 us -> none  [on_device(): lax.psum(partial_sum.astype(jnp.bfloat16), 'variant').astype(jnp.float32)]
    all_gather x0 -> x7, waiting for transfers between devices: none -> 482 us  [on_device(): lax.all_gather(partial_sum.astype(jnp.bfloat16), 'variant')]
    psum x8, waiting for transfers between devices: 501 us -> 439 us  [on_device(): gradient = lax.psum(grad_part, 'sample') * grad_scale]
  transfers between devices with their start and end apart: 8 -> 15, of which waited for: 8 -> 15; matrix products, arithmetic and copies ran while one was open for 3% -> 5% of each run, Pallas kernels for 0% -> 0%
where the time goes in v1:
time: 1170 us
  waiting for transfers between devices  921 us (79%)
  blocking collectives  93.8 us (8%)
  other arithmetic  73.9 us (6%)
  matrix products  56.4 us (5%)
  between operations  13.6 us (1%)
  local copies, waits for them, and re-layouts  12.6 us (1%)
    all_gather x7, waiting for transfers between devices, on_device(): lax.all_gather(partial_sum.astype(jnp.bfloat16), 'variant')  482 us
    psum x8, waiting for transfers between devices, on_device(): gradient = lax.psum(grad_part, 'sample') * grad_scale  439 us
    psum x8, blocking collectives, trait_power(): return lax.psum(squares, 'trait')  93.8 us
    scatter-add x8, other arithmetic, on_device(): counts = jnp.zeros((local_rows,), jnp.float32).at[batch_rows[step]].add(1.0)  60.9 us
    dot_general x7, matrix products, on_device(): lax.dot_general(dosages, weights_low, (((1,), (1,)), ((), ())), preferred...  28.3 us
    dot_general x8, matrix products, on_device(): lax.dot_general(misfit, dosages, (((0,), (0,)), ((), ())), preferred_elem...  28.1 us
  transfers between devices with their start and end apart: 15, of which 15 were waited for; matrix products, arithmetic and copies ran while one was open for 5% of the time, Pallas kernels for 0%

profile of v1, /device:TPU:1, one launch (start us, length us, event | category | flops | bytes accessed | tf_op | source)
XLA Modules:
  0.0 1172.5 jit_solution(12466238087528474747)
XLA Ops:
  7.7 7.6 scatter_custom_fusion
  19.0 57.6 %all-reduce.9.cloned.1.call-done = f32[16,2048]{1,0:T(8,128)} async-done(((f32[16,2048]{1,0:T(8,128)}), f32[16,2048]{1,0:T(8,128)}) %all-reduce.9.cloned.1.call-update) | async-done | bytes 131088 | tf_op jit(solution)/shard_map/psum | solution.py:46
  77.5 11.7 %psum.113 = f32[2048]{0:T(1024)S(1)} all-reduce(f32[2048]{0:T(1024)S(1)} %multiply_reduce_fusion.7), channel_id=1, replica_groups=mesh['sample'=4,'variant'=32,'trait'=4] {'trait'}, use_global_device_ids=true, to_apply=%region_4.5 | all-reduce | flops 2048 | bytes 16384 | tf_op jit(solution)/shard_map/psum | solution.py:12
  93.4 7.6 scatter_custom_fusion.1
  101.0 68.9 %all-gather.15.cloned.1.call-done = bf16[32768,16]{0,1:T(8,128)(2,1)} async-done(((bf16[1024,16]{0,1:T(8,128)(2,1)}), bf16[32768,16]{0,1:T(8,128)(2,1)}) %all-gather.15.cloned.1.call-update) | async-done | bytes 1048592 | tf_op jit(solution)/shard_map/all_gather | solution.py:37
  175.7 54.5 %all-reduce.11.cloned.1.call-done = f32[16,2048]{1,0:T(8,128)} async-done(((f32[16,2048]{1,0:T(8,128)}), f32[16,2048]{1,0:T(8,128)}) %all-reduce.11.cloned.1.call-update) | async-done | bytes 131088 | tf_op jit(solution)/shard_map/psum | solution.py:46
  231.1 11.7 %psum.115 = f32[2048]{0:T(1024)S(1)} all-reduce(f32[2048]{0:T(1024)S(1)} %get-tuple-element.11), channel_id=1, replica_groups=mesh['sample'=4,'variant'=32,'trait'=4] {'trait'}, use_global_device_ids=true, to_apply=%region_9.10 | all-reduce | flops 2048 | bytes 16384 | tf_op jit(solution)/shard_map/psum | solution.py:12
  246.9 7.6 scatter_custom_fusion.2
  254.6 68.9 %all-gather.17.cloned.1.call-done = bf16[32768,16]{0,1:T(8,128)(2,1)} async-done(((bf16[1024,16]{0,1:T(8,128)(2,1)}), bf16[32768,16]{0,1:T(8,128)(2,1)}) %all-gather.17.cloned.1.call-update) | async-done | bytes 1048592 | tf_op jit(solution)/shard_map/all_gather | solution.py:37
  329.2 54.5 %all-reduce.13.cloned.1.call-done = f32[16,2048]{1,0:T(8,128)} async-done(((f32[16,2048]{1,0:T(8,128)}), f32[16,2048]{1,0:T(8,128)}) %all-reduce.13.cloned.1.call-update) | async-done | bytes 131088 | tf_op jit(solution)/shard_map/psum | solution.py:46
  384.7 11.7 %psum.117 = f32[2048]{0:T(1024)S(1)} all-reduce(f32[2048]{0:T(1024)S(1)} %multiply_reduce_fusion.5), channel_id=1, replica_groups=mesh['sample'=4,'variant'=32,'trait'=4] {'trait'}, use_global_device_ids=true, to_apply=%region_14.15 | all-reduce | flops 2048 | bytes 16384 | tf_op jit(solution)/shard_map/psum | solution.py:12
  396.4 4.1 fusion.2
  400.8 7.6 scatter_custom_fusion.3
  408.4 68.7 %all-gather.19.cloned.1.call-done = bf16[32768,16]{0,1:T(8,128)(2,1)} async-done(((bf16[1024,16]{0,1:T(8,128)(2,1)}), bf16[32768,16]{0,1:T(8,128)(2,1)}) %all-gather.19.cloned.1.call-update) | async-done | bytes 1048592 | tf_op jit(solution)/shard_map/all_gather | solution.py:37
  482.9 54.5 %all-reduce.15.cloned.1.call-done = f32[16,2048]{1,0:T(8,128)} async-done(((f32[16,2048]{1,0:T(8,128)}), f32[16,2048]{1,0:T(8,128)}) %all-reduce.15.cloned.1.call-update) | async-done | bytes 131088 | tf_op jit(solution)/shard_map/psum | solution.py:46
  538.3 11.7 %psum.119 = f32[2048]{0:T(1024)S(1)} all-reduce(f32[2048]{0:T(1024)S(1)} %get-tuple-element.9), channel_id=1, replica_groups=mesh['sample'=4,'variant'=32,'trait'=4] {'trait'}, use_global_device_ids=true, to_apply=%region_19.20 | all-reduce | flops 2048 | bytes 16384 | tf_op jit(solution)/shard_map/psum | solution.py:12
  554.1 7.6 scatter_custom_fusion.4
  561.8 68.9 %all-gather.21.cloned.1.call-done = bf16[32768,16]{0,1:T(8,128)(2,1)} async-done(((bf16[1024,16]{0,1:T(8,128)(2,1)}), bf16[32768,16]{0,1:T(8,128)(2,1)}) %all-gather.21.cloned.1.call-update) | async-done | bytes 1048592 | tf_op jit(solution)/shard_map/all_gather | solution.py:37
  636.4 54.5 %all-reduce.17.cloned.1.call-done = f32[16,2048]{1,0:T(8,128)} async-done(((f32[16,2048]{1,0:T(8,128)}), f32[16,2048]{1,0:T(8,128)}) %all-reduce.17.cloned.1.call-update) | async-done | bytes 131088 | tf_op jit(solution)/shard_map/psum | solution.py:46
  691.9 11.7 %psum.121 = f32[2048]{0:T(1024)S(1)} all-reduce(f32[2048]{0:T(1024)S(1)} %multiply_reduce_fusion.3), channel_id=1, replica_groups=mesh['sample'=4,'variant'=32,'trait'=4] {'trait'}, use_global_device_ids=true, to_apply=%region_24.25 | all-reduce | flops 2048 | bytes 16384 | tf_op jit(solution)/shard_map/psum | solution.py:12
  707.8 7.6 scatter_custom_fusion.5
  715.4 68.9 %all-gather.23.cloned.1.call-done = bf16[32768,16]{0,1:T(8,128)(2,1)} async-done(((bf16[1024,16]{0,1:T(8,128)(2,1)}), bf16[32768,16]{0,1:T(8,128)(2,1)}) %all-gather.23.cloned.1.call-update) | async-done | bytes 1048592 | tf_op jit(solution)/shard_map/all_gather | solution.py:37
  790.1 54.5 %all-reduce.19.cloned.1.call-done = f32[16,2048]{1,0:T(8,128)} async-done(((f32[16,2048]{1,0:T(8,128)}), f32[16,2048]{1,0:T(8,128)}) %all-reduce.19.cloned.1.call-update) | async-done | bytes 131088 | tf_op jit(solution)/shard_map/psum | solution.py:46
  845.5 11.7 %psum.123 = f32[2048]{0:T(1024)S(1)} all-reduce(f32[2048]{0:T(1024)S(1)} %get-tuple-element.7), channel_id=1, replica_groups=mesh['sample'=4,'variant'=32,'trait'=4] {'trait'}, use_global_device_ids=true, to_apply=%region_29.30 | all-reduce | flops 2048 | bytes 16384 | tf_op jit(solution)/shard_map/psum | solution.py:12
  861.6 7.6 scatter_custom_fusion.6
  869.2 68.7 %all-gather.25.cloned.1.call-done = bf16[32768,16]{0,1:T(8,128)(2,1)} async-done(((bf16[1024,16]{0,1:T(8,128)(2,1)}), bf16[32768,16]{0,1:T(8,128)(2,1)}) %all-gather.25.cloned.1.call-update) | async-done | bytes 1048592 | tf_op jit(solution)/shard_map/all_gather | solution.py:37
  943.6 54.5 %all-reduce.21.cloned.1.call-done = f32[16,2048]{1,0:T(8,128)} async-done(((f32[16,2048]{1,0:T(8,128)}), f32[16,2048]{1,0:T(8,128)}) %all-reduce.21.cloned.1.call-update) | async-done | bytes 131088 | tf_op jit(solution)/shard_map/psum | solution.py:46
  999.1 11.7 %psum.125 = f32[2048]{0:T(1024)S(1)} all-reduce(f32[2048]{0:T(1024)S(1)} %get-tuple-element.5), channel_id=1, replica_groups=mesh['sample'=4,'variant'=32,'trait'=4] {'trait'}, use_global_device_ids=true, to_apply=%region_34.35 | all-reduce | flops 2048 | bytes 16384 | tf_op jit(solution)/shard_map/psum | solution.py:12
  1014.9 7.6 scatter_custom_fusion.7
  1022.5 68.9 %all-gather.27.cloned.1.call-done = bf16[32768,16]{0,1:T(8,128)(2,1)} async-done(((bf16[1024,16]{0,1:T(8,128)(2,1)}), bf16[32768,16]{0,1:T(8,128)(2,1)}) %all-gather.27.cloned.1.call-update) | async-done | bytes 1048592 | tf_op jit(solution)/shard_map/all_gather | solution.py:37
  1097.1 54.5 %all-reduce.23.cloned.1.call-done = f32[16,2048]{1,0:T(8,128)} async-done(((f32[16,2048]{1,0:T(8,128)}), f32[16,2048]{1,0:T(8,128)}) %all-reduce.23.cloned.1.call-update) | async-done | bytes 131088 | tf_op jit(solution)/shard_map/psum | solution.py:46
  1152.6 11.7 %psum.127 = f32[2048]{0:T(1024)S(1)} all-reduce(f32[2048]{0:T(1024)S(1)} %multiply_reduce_fusion), channel_id=1, replica_groups=mesh['sample'=4,'variant'=32,'trait'=4] {'trait'}, use_global_device_ids=true, to_apply=%region_38.39 | all-reduce | flops 2048 | bytes 16384 | tf_op jit(solution)/shard_map/psum | solution.py:12
  (85 shorter events, 79.1 us)
Async XLA Ops:
  6.5 70.0 %all-reduce.9.cloned.1.call-start = ((), (), s32[]{:S(2)}) async-start(), calls=%async_computation | async-start | bytes 262144 | tf_op jit(solution)/shard_map/psum | solution.py:46
  18.9 153.2 %copy-start = (f32[1024,16]{0,1:T(8,128)S(1)}, f32[1024,16]{0,1:T(8,128)}, u32[]{:S(2)}) copy-start(f32[1024,16]{0,1:T(8,128)} %param.4) | copy-start | bytes 196612
  18.9 151.0 %all-gather.15.cloned.1.call-start = ((), (), s32[]{:S(2)}) async-start(), calls=%async_computation.8 | async-start | bytes 1081344 | tf_op jit(solution)/shard_map/all_gather | solution.py:37
  93.3 136.9 %copy-start.1 = (f32[16,2048]{1,0:T(8,128)S(1)}, f32[16,2048]{1,0:T(8,128)}, u32[]{:S(2)}) copy-start(f32[16,2048]{1,0:T(8,128)} %all-reduce.9.cloned.1.call-done) | copy-start | bytes 393220
  93.3 136.8 %all-reduce.11.cloned.1.call-start = ((), (), s32[]{:S(2)}) async-start(), calls=%async_computation.1 | async-start | bytes 262144 | tf_op jit(solution)/shard_map/psum | solution.py:46
  175.6 147.9 %all-gather.17.cloned.1.call-start = ((), (), s32[]{:S(2)}) async-start(), calls=%async_computation.9 | async-start | bytes 1081344 | tf_op jit(solution)/shard_map/all_gather | solution.py:37
  246.9 136.8 %all-reduce.13.cloned.1.call-start = ((), (), s32[]{:S(2)}) async-start(), calls=%async_computation.2 | async-start | bytes 262144 | tf_op jit(solution)/shard_map/psum | solution.py:46
  329.2 147.9 %all-gather.19.cloned.1.call-start = ((), (), s32[]{:S(2)}) async-start(), calls=%async_computation.10 | async-start | bytes 1081344 | tf_op jit(solution)/shard_map/all_gather | solution.py:37
  400.5 136.8 %copy-start.2 = (f32[16,2048]{1,0:T(8,128)S(1)}, f32[16,2048]{1,0:T(8,128)}, u32[]{:S(2)}) copy-start(f32[16,2048]{1,0:T(8,128)} %all-reduce.13.cloned.1.call-done) | copy-start | bytes 393220
  400.5 136.8 %all-reduce.15.cloned.1.call-start = ((), (), s32[]{:S(2)}) async-start(), calls=%async_computation.3 | async-start | bytes 262144 | tf_op jit(solution)/shard_map/psum | solution.py:46
  482.8 147.9 %all-gather.21.cloned.1.call-start = ((), (), s32[]{:S(2)}) async-start(), calls=%async_computation.11 | async-start | bytes 1081344 | tf_op jit(solution)/shard_map/all_gather | solution.py:37
  554.1 136.8 %all-reduce.17.cloned.1.call-start = ((), (), s32[]{:S(2)}) async-start(), calls=%async_computation.4 | async-start | bytes 262144 | tf_op jit(solution)/shard_map/psum | solution.py:46
  636.4 147.9 %all-gather.23.cloned.1.call-start = ((), (), s32[]{:S(2)}) async-start(), calls=%async_computation.12 | async-start | bytes 1081344 | tf_op jit(solution)/shard_map/all_gather | solution.py:37
  707.7 136.8 %copy-start.3 = (f32[16,2048]{1,0:T(8,128)S(1)}, f32[16,2048]{1,0:T(8,128)}, u32[]{:S(2)}) copy-start(f32[16,2048]{1,0:T(8,128)} %all-reduce.17.cloned.1.call-done) | copy-start | bytes 393220
  707.7 136.8 %all-reduce.19.cloned.1.call-start = ((), (), s32[]{:S(2)}) async-start(), calls=%async_computation.5 | async-start | bytes 262144 | tf_op jit(solution)/shard_map/psum | solution.py:46
  790.0 147.9 %all-gather.25.cloned.1.call-start = ((), (), s32[]{:S(2)}) async-start(), calls=%async_computation.13 | async-start | bytes 1081344 | tf_op jit(solution)/shard_map/all_gather | solution.py:37
  861.3 136.8 %all-reduce.21.cloned.1.call-start = ((), (), s32[]{:S(2)}) async-start(), calls=%async_computation.6 | async-start | bytes 262144 | tf_op jit(solution)/shard_map/psum | solution.py:46
  943.6 147.9 %all-gather.27.cloned.1.call-start = ((), (), s32[]{:S(2)}) async-start(), calls=%async_computation.14 | async-start | bytes 1081344 | tf_op jit(solution)/shard_map/all_gather | solution.py:37
  1014.8 136.8 %all-reduce.23.cloned.1.call-start = ((), (), s32[]{:S(2)}) async-start(), calls=%async_computation.7 | async-start | bytes 262144 | tf_op jit(solution)/shard_map/psum | solution.py:46
Sparse Core Ops, SparseCore 0:
  19.0 57.4 all-reduce.8
  93.5 76.4 all-gather.14
  175.7 54.3 all-reduce.10
  247.0 76.4 all-gather.16
  329.3 54.3 all-reduce.12
  400.6 76.4 all-gather.18
  482.9 54.3 all-reduce.14
  554.2 76.4 all-gather.20
  636.5 54.3 all-reduce.16
  707.8 76.4 all-gather.22
  790.1 54.3 all-reduce.18
  861.4 76.4 all-gather.24
  943.7 54.3 all-reduce.20
  1015.0 76.4 all-gather.26
  1097.2 54.3 all-reduce.22
